TPU v7x, 32 devices: a whole 2x2x4 slice. The times are simulated.
32 devices in a mesh: dp: 8 (over z, x), tensor: 4 (over y, core).
Axes of the slice: x: 2, y: 2, z: 4, core: 2. Of those that a mesh axis runs over, the one named last changes fastest.
Arguments:
- tokens: bfloat16 [8192, 2048], P(('dp', 'tensor')), may hold values from -6 to 6
- pieces: int32 [8192], P('dp'), may hold values from 0 to 32, as said below
- positions: int32 [8192], P('dp'), may hold values from 0 to 798, as said below
- cotangent: bfloat16 [8192, 2048], P(('dp', 'tensor')), may hold values from -6 to 6
- attn_norm: float32 [2048], P('dp'), may hold values from 0.25 to 1.75
- w_query: float32 [2048, 2048], P('dp', 'tensor'), may hold values from -0.125 to 0.125
- w_key: float32 [2048, 512], P('dp', 'tensor'), may hold values from -0.125 to 0.125
- w_value: float32 [2048, 512], P('dp', 'tensor'), may hold values from -0.125 to 0.125
- w_out: float32 [2048, 2048], P('tensor', 'dp'), may hold values from -0.75 to 0.75
- mlp_norm: float32 [2048], P('dp'), may hold values from 0.25 to 1.75
- w_gate: float32 [2048, 8192], P('dp', 'tensor'), may hold values from -0.125 to 0.125
- w_up: float32 [2048, 8192], P('dp', 'tensor'), may hold values from -0.125 to 0.125
- w_down: float32 [8192, 2048], P('tensor', 'dp'), may hold values from -0.0625 to 0.0625
Outputs:
- output: bfloat16 [8192, 2048], P(('dp', 'tensor'))
- input_grad: float32 [8192, 2048], P(('dp', 'tensor'))
- grad_attn_norm: float32 [2048], P('dp')
- grad_w_query: float32 [2048, 2048], P('dp', 'tensor')
- grad_w_key: float32 [2048, 512], P('dp', 'tensor')
- grad_w_value: float32 [2048, 512], P('dp', 'tensor')
- grad_w_out: float32 [2048, 2048], P('tensor', 'dp')
- grad_mlp_norm: float32 [2048], P('dp')
- grad_w_gate: float32 [2048, 8192], P('dp', 'tensor')
- grad_w_up: float32 [2048, 8192], P('dp', 'tensor')
- grad_w_down: float32 [8192, 2048], P('tensor', 'dp')
Inputs may be any that keep to these rules, and one draw needn't show every extreme that they name: `pieces`: each aligned run of 256 tokens is text (0) or one picture piece numbered 1 + the run's index among all runs; the last run of every sequence is a picture piece. `positions`: A text token's position is its index within its sequence of 1024 tokens; the t-th token of a picture piece takes the index of the piece's first token + t // 16 + t % 16.
All inputs are finite; a program needn't handle non-finite values.
Results may differ from a plain program's by a relative error of at most 0.02.
Values may be sent and summed in bfloat16 or wider, within the bound.
No kernel may reach another device: no remote copies, remote signals or barrier semaphores. Data moves between devices by JAX's collectives and lax.ppermute only.
A program may use at most 256 MiB of HBM per device.

v0:
```python
from functools import reduce
import math
import jax
import jax.numpy as jnp
from jax import lax
from jax.sharding import PartitionSpec as P

HEADS = 32
KV_HEADS = 8
HEAD_DIM = 64


def rotary_angles(positions, head_size):
    half = head_size // 2
    base = jnp.power(500000.0, -(jnp.arange(half, dtype=jnp.float32) * 2.0 / head_size))
    wavelen = 2.0 * math.pi / base
    smooth = (8192.0 / wavelen - 1.0) / 3.0
    blended = (1.0 - smooth) * base / 32.0 + smooth * base
    scaled = jnp.where(wavelen > 8192.0, base / 32.0, jnp.where(wavelen < 2048.0, base, blended))
    return positions.astype(jnp.float32)[:, None] * scaled[None, :]


def rotate(field, angles):
    half = field.shape[-1] // 2
    cosine = jnp.cos(angles)[:, None, :]
    sine = jnp.sin(angles)[:, None, :]
    first = field[..., :half]
    second = field[..., half:]
    return jnp.concatenate(
        [first * cosine - second * sine, second * cosine + first * sine], axis=-1
    )


def normalize(residual, gain):
    inverse = lax.rsqrt(jnp.mean(residual * residual, axis=-1, keepdims=True) + 1e-05)
    return ((residual * inverse * gain.astype(jnp.float32)).astype(jnp.bfloat16), inverse)


def normalize_back(grad_normed, residual, inverse, gain):
    scaled = residual * inverse
    grad_gain = jnp.sum(grad_normed * scaled, axis=0)
    weighted = grad_normed * gain.astype(jnp.float32)
    grad_residual = inverse * (
        weighted - scaled * jnp.mean(weighted * scaled, axis=-1, keepdims=True)
    )
    return (grad_residual, grad_gain)


def row_product(left, right):
    return jnp.dot(left, right, preferred_element_type=jnp.float32)


def back_product(lefts, rights):
    parts = [
        lax.dot_general(left, right, (((1,), (1,)), ((), ())), preferred_element_type=jnp.float32)
        for left, right in zip(lefts, rights)
    ]
    return reduce(jnp.add, parts)


def across_rows(left, right):
    return lax.dot_general(
        left, right, (((0,), (0,)), ((), ())), preferred_element_type=jnp.float32
    )


def masked_scores(block_query, keys, pieces, first, scale_factor):
    count = block_query.shape[0]
    length = keys.shape[0]
    scores = (
        jnp.einsum("qgrd,kgd->grqk", block_query, keys, preferred_element_type=jnp.float32)
        * scale_factor
    )
    rows = first + jnp.arange(count)[:, None]
    columns = jnp.arange(length)[None, :]
    owner = pieces[first : first + count][:, None]
    allowed = (columns <= rows) | (owner == pieces[None, :]) & (owner != 0)
    return jnp.where(allowed, scores, -1e30)


def attend(query, keys, values, pieces, scale_factor):
    length = query.shape[0]
    block = min(512, length)
    attended_parts = []
    total_parts = []
    for first in range(0, length, block):
        scores = masked_scores(query[first : first + block], keys, pieces, first, scale_factor)
        peak = jnp.max(scores, axis=-1, keepdims=True)
        exponent = jnp.exp(scores - peak)
        total = jnp.sum(exponent, axis=-1, keepdims=True)
        probs = (exponent / total).astype(jnp.bfloat16)
        attended_parts.append(
            jnp.einsum("grqk,kgd->qgrd", probs, values, preferred_element_type=jnp.float32).astype(
                jnp.bfloat16
            )
        )
        total_parts.append(peak + jnp.log(total))
    return (jnp.concatenate(attended_parts, axis=0), jnp.concatenate(total_parts, axis=2))


def attend_back(query, keys, values, grad_attended, log_totals, pieces, scale_factor):
    length = query.shape[0]
    block = min(512, length)
    grad_query_parts = []
    grad_keys = jnp.zeros(keys.shape, jnp.float32)
    grad_values = jnp.zeros(values.shape, jnp.float32)
    for first in range(0, length, block):
        block_query = query[first : first + block]
        block_grad = grad_attended[first : first + block]
        scores = masked_scores(block_query, keys, pieces, first, scale_factor)
        probs = jnp.exp(scores - log_totals[:, :, first : first + block])
        probs_low = probs.astype(jnp.bfloat16)
        grad_probs = jnp.einsum(
            "qgrd,kgd->grqk", block_grad, values, preferred_element_type=jnp.float32
        )
        inner = jnp.sum(probs * grad_probs, axis=-1, keepdims=True)
        grad_scores = (probs * (grad_probs - inner)).astype(jnp.bfloat16)
        grad_query_parts.append(
            jnp.einsum("grqk,kgd->qgrd", grad_scores, keys, preferred_element_type=jnp.float32)
            * scale_factor
        )
        grad_keys = (
            grad_keys
            + jnp.einsum(
                "grqk,qgrd->kgd", grad_scores, block_query, preferred_element_type=jnp.float32
            )
            * scale_factor
        )
        grad_values = grad_values + jnp.einsum(
            "grqk,qgrd->kgd", probs_low, block_grad, preferred_element_type=jnp.float32
        )
    return (jnp.concatenate(grad_query_parts, axis=0), grad_keys, grad_values)


def gather_rows(rows):
    return lax.all_gather(rows, "tensor", axis=0, tiled=True)


def gather_grads(rows):
    return lax.all_gather(rows, "tensor", axis=0, tiled=True)


def local(
    tokens,
    pieces,
    positions,
    cotangent,
    attn_norm,
    w_query,
    w_key,
    w_value,
    w_out,
    mlp_norm,
    w_gate,
    w_up,
    w_down,
):
    attn_gain, query_weight, key_weight, value_weight, out_weight = (
        lax.all_gather(attn_norm.astype(jnp.bfloat16), "dp", axis=0, tiled=True),
        lax.all_gather(w_query.astype(jnp.bfloat16), "dp", axis=0, tiled=True),
        lax.all_gather(w_key.astype(jnp.bfloat16), "dp", axis=0, tiled=True),
        lax.all_gather(w_value.astype(jnp.bfloat16), "dp", axis=0, tiled=True),
        lax.all_gather(w_out.astype(jnp.bfloat16), "dp", axis=1, tiled=True),
    )
    mlp_gain, gate_weight, up_weight, down_weight = (
        lax.all_gather(mlp_norm.astype(jnp.bfloat16), "dp", axis=0, tiled=True),
        lax.all_gather(w_gate.astype(jnp.bfloat16), "dp", axis=0, tiled=True),
        lax.all_gather(w_up.astype(jnp.bfloat16), "dp", axis=0, tiled=True),
        lax.all_gather(w_down.astype(jnp.bfloat16), "dp", axis=1, tiled=True),
    )
    group = HEADS // KV_HEADS
    key_heads = key_weight.shape[1] // HEAD_DIM
    scale_factor = HEAD_DIM ** (-0.5)
    residual = tokens.astype(jnp.float32)
    normed_one, inverse_one = normalize(residual, attn_gain)
    normed_full = gather_rows(normed_one)
    length = normed_full.shape[0]
    angles = rotary_angles(positions, HEAD_DIM)
    query = jnp.dot(normed_full, query_weight, preferred_element_type=jnp.float32).reshape(
        length, -1, HEAD_DIM
    )
    query = rotate(query, angles).astype(jnp.bfloat16).reshape(length, key_heads, group, HEAD_DIM)
    keys = jnp.dot(normed_full, key_weight, preferred_element_type=jnp.float32).reshape(
        length, key_heads, HEAD_DIM
    )
    keys = rotate(keys, angles).astype(jnp.bfloat16)
    values = jnp.dot(normed_full, value_weight, preferred_element_type=jnp.float32).astype(
        jnp.bfloat16
    )
    values = values.reshape(length, key_heads, HEAD_DIM)
    attended, log_totals = attend(query, keys, values, pieces, scale_factor)
    attended_flat = attended.reshape(length, -1)
    middle = residual + lax.psum_scatter(
        row_product(attended_flat, out_weight), "tensor", scatter_dimension=0, tiled=True
    )
    normed_two, inverse_two = normalize(middle, mlp_gain)
    normed_full_two = gather_rows(normed_two)
    gate = jnp.dot(normed_full_two, gate_weight, preferred_element_type=jnp.float32)
    up = jnp.dot(normed_full_two, up_weight, preferred_element_type=jnp.float32)
    gate_sigmoid = jax.nn.sigmoid(gate)
    activated = gate * gate_sigmoid
    hidden = (activated * up).astype(jnp.bfloat16)
    result = middle + lax.psum_scatter(
        row_product(hidden, down_weight).astype(jnp.bfloat16),
        "tensor",
        scatter_dimension=0,
        tiled=True,
    ).astype(jnp.float32)
    output = result.astype(jnp.bfloat16)
    mlp_gain, gate_weight, up_weight, down_weight = (
        lax.all_gather(mlp_norm.astype(jnp.bfloat16), "dp", axis=0, tiled=True),
        lax.all_gather(w_gate.astype(jnp.bfloat16), "dp", axis=0, tiled=True),
        lax.all_gather(w_up.astype(jnp.bfloat16), "dp", axis=0, tiled=True),
        lax.all_gather(w_down.astype(jnp.bfloat16), "dp", axis=1, tiled=True),
    )
    grad_out = cotangent.astype(jnp.float32)
    grad_out_full = gather_grads(cotangent)
    grad_hidden = lax.dot_general(
        grad_out_full, down_weight, (((1,), (1,)), ((), ())), preferred_element_type=jnp.float32
    )
    grad_gate = (grad_hidden * up * gate_sigmoid * (1.0 + gate * (1.0 - gate_sigmoid))).astype(
        jnp.bfloat16
    )
    grad_up = (grad_hidden * activated).astype(jnp.bfloat16)
    grad_w_down = across_rows(hidden, grad_out_full)
    grad_w_gate = across_rows(normed_full_two, grad_gate)
    grad_w_up = across_rows(normed_full_two, grad_up)
    grad_normed_two = lax.psum_scatter(
        back_product((grad_gate, grad_up), (gate_weight, up_weight)),
        "tensor",
        scatter_dimension=0,
        tiled=True,
    )
    grad_middle_norm, grad_gain_two = normalize_back(grad_normed_two, middle, inverse_two, mlp_gain)
    grad_middle = grad_out + grad_middle_norm
    gain_two_part, grad_w_gate, grad_w_up, grad_w_down = (
        lax.psum_scatter(
            grad_gain_two.astype(jnp.bfloat16), "dp", scatter_dimension=0, tiled=True
        ).astype(jnp.float32),
        lax.psum_scatter(
            grad_w_gate.astype(jnp.bfloat16), "dp", scatter_dimension=0, tiled=True
        ).astype(jnp.float32),
        lax.psum_scatter(
            grad_w_up.astype(jnp.bfloat16), "dp", scatter_dimension=0, tiled=True
        ).astype(jnp.float32),
        lax.psum_scatter(
            grad_w_down.astype(jnp.bfloat16), "dp", scatter_dimension=1, tiled=True
        ).astype(jnp.float32),
    )
    grad_branch_full = gather_grads(grad_middle.astype(jnp.bfloat16))
    attn_gain, query_weight, key_weight, value_weight, out_weight = (
        lax.all_gather(attn_norm.astype(jnp.bfloat16), "dp", axis=0, tiled=True),
        lax.all_gather(w_query.astype(jnp.bfloat16), "dp", axis=0, tiled=True),
        lax.all_gather(w_key.astype(jnp.bfloat16), "dp", axis=0, tiled=True),
        lax.all_gather(w_value.astype(jnp.bfloat16), "dp", axis=0, tiled=True),
        lax.all_gather(w_out.astype(jnp.bfloat16), "dp", axis=1, tiled=True),
    )
    grad_attended = lax.dot_general(
        grad_branch_full, out_weight, (((1,), (1,)), ((), ())), preferred_element_type=jnp.float32
    )
    grad_attended = grad_attended.astype(jnp.bfloat16).reshape(length, key_heads, group, HEAD_DIM)
    grad_query_rot, grad_keys_rot, grad_values = attend_back(
        query, keys, values, grad_attended, log_totals, pieces, scale_factor
    )
    grad_query = (
        rotate(grad_query_rot.reshape(length, -1, HEAD_DIM), -angles)
        .astype(jnp.bfloat16)
        .reshape(length, -1)
    )
    grad_keys = rotate(grad_keys_rot, -angles).astype(jnp.bfloat16).reshape(length, -1)
    grad_values = grad_values.astype(jnp.bfloat16).reshape(length, -1)
    grad_normed_one = lax.psum_scatter(
        back_product(
            (grad_query, grad_keys, grad_values), (query_weight, key_weight, value_weight)
        ).astype(jnp.bfloat16),
        "tensor",
        scatter_dimension=0,
        tiled=True,
    ).astype(jnp.float32)
    grad_input_norm, grad_gain_one = normalize_back(
        grad_normed_one, residual, inverse_one, attn_gain
    )
    input_grad = grad_middle + grad_input_norm
    grad_w_out = across_rows(attended_flat, grad_branch_full)
    grad_w_query = across_rows(normed_full, grad_query)
    grad_w_key = across_rows(normed_full, grad_keys)
    grad_w_value = across_rows(normed_full, grad_values)
    gain_one_part, grad_w_query, grad_w_key, grad_w_value, grad_w_out = (
        lax.psum_scatter(
            grad_gain_one.astype(jnp.bfloat16), "dp", scatter_dimension=0, tiled=True
        ).astype(jnp.float32),
        lax.psum_scatter(
            grad_w_query.astype(jnp.bfloat16), "dp", scatter_dimension=0, tiled=True
        ).astype(jnp.float32),
        lax.psum_scatter(
            grad_w_key.astype(jnp.bfloat16), "dp", scatter_dimension=0, tiled=True
        ).astype(jnp.float32),
        lax.psum_scatter(
            grad_w_value.astype(jnp.bfloat16), "dp", scatter_dimension=0, tiled=True
        ).astype(jnp.float32),
        lax.psum_scatter(
            grad_w_out.astype(jnp.bfloat16), "dp", scatter_dimension=1, tiled=True
        ).astype(jnp.float32),
    )
    gain_one, gain_two = lax.psum((gain_one_part, gain_two_part), "tensor")
    return (
        output,
        input_grad,
        gain_one,
        grad_w_query,
        grad_w_key,
        grad_w_value,
        grad_w_out,
        gain_two,
        grad_w_gate,
        grad_w_up,
        grad_w_down,
    )


def solution(mesh):
    return jax.shard_map(
        local,
        mesh=mesh,
        in_specs=(
            P(("dp", "tensor"), None),
            P("dp"),
            P("dp"),
            P(("dp", "tensor"), None),
            P("dp"),
            P("dp", "tensor"),
            P("dp", "tensor"),
            P("dp", "tensor"),
            P("tensor", "dp"),
            P("dp"),
            P("dp", "tensor"),
            P("dp", "tensor"),
            P("tensor", "dp"),
        ),
        out_specs=(
            P(("dp", "tensor"), None),
            P(("dp", "tensor"), None),
            P("dp"),
            P("dp", "tensor"),
            P("dp", "tensor"),
            P("dp", "tensor"),
            P("tensor", "dp"),
            P("dp"),
            P("dp", "tensor"),
            P("dp", "tensor"),
            P("tensor", "dp"),
        ),
        check_vma=False,
    )
```

profile of v0, /device:TPU:0, one launch (start us, length us, event | category | flops | bytes accessed | tf_op | source)
XLA Modules:
  0.0 1690.8 jit_solution(2839369991846664020)
XLA Ops:
  9.6 22.3 %all-gather = bf16[8,1,256]{2,1,0:T(2,128)(2,1)S(1)} all-gather(bf16[1,1,256]{2,1,0:T(2,128)(2,1)S(1)} %reshape.227), channel_id=1, replica_groups=mesh['dp'=8,'tensor'=4] {'dp'}, dimensions={0}, use_global_device_ids=true | all-gather | bytes 4608 | tf_op jit(solution)/shard_map/all_gather | solution.py:159
  36.8 31.5 %all_gather.50 = bf16[2048,128]{1,0:T(8,128)(2,1)S(1)} all-gather(bf16[256,128]{1,0:T(8,128)(2,1)S(1)} %convert_element_type.198), channel_id=1, replica_groups=mesh['dp'=8,'tensor'=4] {'dp'}, dimensions={0}, use_global_device_ids=true | all-gather | bytes 589824 | tf_op jit(solution)/shard_map/all_gather | solution.py:162
  68.3 32.4 %all_gather.51 = bf16[2048,128]{1,0:T(8,128)(2,1)S(1)} all-gather(bf16[256,128]{1,0:T(8,128)(2,1)S(1)} %convert_element_type.200), channel_id=1, replica_groups=mesh['dp'=8,'tensor'=4] {'dp'}, dimensions={0}, use_global_device_ids=true | all-gather | bytes 589824 | tf_op jit(solution)/shard_map/all_gather | solution.py:161
  107.3 12.4 all-gather.14.cloned.1.call-done
  184.0 18.3 %all-gather.1 = bf16[8,1,256]{2,1,0:T(2,128)(2,1)S(1)} all-gather(bf16[1,1,256]{2,1,0:T(2,128)(2,1)S(1)} %reshape.229), channel_id=1, replica_groups=mesh['dp'=8,'tensor'=4] {'dp'}, dimensions={0}, use_global_device_ids=true | all-gather | bytes 4608 | tf_op jit(solution)/shard_map/all_gather | solution.py:166
  202.3 49.1 %reduce-scatter.12.cloned.1.call-done = f32[256,2048]{1,0:T(8,128)} async-done(((f32[1024,2048]{1,0:T(8,128)}), f32[256,2048]{1,0:T(8,128)}) %reduce-scatter.12.cloned.1.call-update) | async-done | bytes 2097168 | tf_op jit(solution)/shard_map/reduce_scatter | solution.py:193
  261.2 117.3 %all-gather.22.cloned.1.call-done = bf16[2048,2048]{1,0:T(8,128)(2,1)} async-done(((bf16[256,2048]{1,0:T(8,128)(2,1)}), bf16[2048,2048]{1,0:T(8,128)(2,1)}) %all-gather.22.cloned.1.call-update) | async-done | bytes 8388624 | tf_op jit(solution)/shard_map/all_gather | solution.py:168
  378.5 34.7 %all-gather.18.cloned.1.call-done = bf16[1024,2048]{1,0:T(8,128)(2,1)} async-done(((bf16[256,2048]{1,0:T(8,128)(2,1)}), bf16[1024,2048]{1,0:T(8,128)(2,1)}) %all-gather.18.cloned.1.call-update) | async-done | bytes 4194320 | tf_op jit(solution)/shard_map/all_gather | solution.py:136
  413.1 14.7 fusion.65
  427.9 112.4 %all-gather.20.cloned.1.call-done = bf16[2048,2048]{1,0:T(8,128)(2,1)} async-done(((bf16[256,2048]{1,0:T(8,128)(2,1)}), bf16[2048,2048]{1,0:T(8,128)(2,1)}) %all-gather.20.cloned.1.call-update) | async-done | bytes 8388624 | tf_op jit(solution)/shard_map/all_gather | solution.py:167
  540.3 14.5 fusion.64
  554.9 19.7 %all-gather.26.cloned.1.call-done = bf16[1024,2048]{1,0:T(8,128)(2,1)} async-done(((bf16[256,2048]{1,0:T(8,128)(2,1)}), bf16[1024,2048]{1,0:T(8,128)(2,1)}) %all-gather.26.cloned.1.call-update) | async-done | bytes 4194320 | tf_op jit(solution)/shard_map/all_gather | solution.py:140
  574.6 127.6 %all-gather.24.cloned.1.call-done = bf16[2048,2048]{1,0:T(8,128)(2,1)} async-done(((bf16[2048,256]{1,0:T(8,128)(2,1)}), bf16[2048,2048]{1,0:T(8,128)(2,1)}) %all-gather.24.cloned.1.call-update) | async-done | bytes 8388624 | tf_op jit(solution)/shard_map/all_gather | solution.py:169
  702.2 21.9 %multiply_convert_fusion = (bf16[1024,2048]{1,0:T(8,128)(2,1)}, bf16[1024,2048]{1,0:T(8,128)(2,1)}, bf16[1024,2048]{1,0:T(8,128)(2,1)}) fusion(f32[1024,2048]{1,0:T(8,128)} %fusion.64, f32[1024,2048]{1,0:T(8,128)} %fusion.65, bf16[1024,2048]{1,0:T(8,128)(2,1)} %all-gather.26.cloned.1.call-done, bf16[2048,2048]{1,0:T(8,128)(2,1)} %all-gather.24.cloned.1.call-done), kind=kOutput, calls=%fused_computation.27 | convolution fusion | flops 8621391872 | bytes 41943040 | tf_op jit(solution)/shard_map/dot_general | solution.py:218
  724.0 13.1 fusion.66
  737.2 13.6 convolution_add_fusion
  750.9 69.7 %reduce-scatter.16.cloned.1.call-done = f32[256,2048]{1,0:T(8,128)} async-done(((f32[1024,2048]{1,0:T(8,128)}), f32[256,2048]{1,0:T(8,128)}) %reduce-scatter.16.cloned.1.call-update) | async-done | bytes 2097168 | tf_op jit(solution)/shard_map/reduce_scatter | solution.py:228
  825.7 14.3 convolution_convert_fusion.1
  840.1 14.1 convolution_convert_fusion.2
  854.3 14.2 convolution_convert_fusion
  894.8 15.3 fusion
  936.0 12.2 fusion.5
  986.2 13.9 convolution_convert_fusion.3
  1014.2 147.4 %reduce-scatter.28.cloned.1.call-done = bf16[256,2048]{1,0:T(8,128)(2,1)} async-done(((bf16[2048,2048]{1,0:T(8,128)(2,1)}), bf16[256,2048]{1,0:T(8,128)(2,1)}) %reduce-scatter.28.cloned.1.call-update) | async-done | bytes 1048592 | tf_op jit(solution)/shard_map/reduce_scatter | solution.py:240
  1164.4 147.7 %reduce-scatter.32.cloned.1.call-done = bf16[2048,256]{1,0:T(8,128)(2,1)} async-done(((bf16[2048,2048]{1,0:T(8,128)(2,1)}), bf16[2048,256]{1,0:T(8,128)(2,1)}) %reduce-scatter.32.cloned.1.call-update) | async-done | bytes 1048592 | tf_op jit(solution)/shard_map/reduce_scatter | solution.py:246
  1314.8 62.8 %reduce-scatter.24.cloned.1.call-done = bf16[256,128]{1,0:T(8,128)(2,1)} async-done(((bf16[2048,128]{1,0:T(8,128)(2,1)}), bf16[256,128]{1,0:T(8,128)(2,1)}) %reduce-scatter.24.cloned.1.call-update) | async-done | bytes 65552 | tf_op jit(solution)/shard_map/reduce_scatter | solution.py:298
  1379.1 63.9 %reduce-scatter.22.cloned.1.call-done = bf16[256,128]{1,0:T(8,128)(2,1)} async-done(((bf16[2048,128]{1,0:T(8,128)(2,1)}), bf16[256,128]{1,0:T(8,128)(2,1)}) %reduce-scatter.22.cloned.1.call-update) | async-done | bytes 65552 | tf_op jit(solution)/shard_map/reduce_scatter | solution.py:295
  1444.5 69.8 %reduce-scatter.26.cloned.1.call-done = bf16[512,256]{1,0:T(8,128)(2,1)} async-done(((bf16[512,2048]{1,0:T(8,128)(2,1)}), bf16[512,256]{1,0:T(8,128)(2,1)}) %reduce-scatter.26.cloned.1.call-update) | async-done | bytes 262160 | tf_op jit(solution)/shard_map/reduce_scatter | solution.py:301
  1516.1 69.0 %reduce-scatter.20.cloned.1.call-done = bf16[256,512]{1,0:T(8,128)(2,1)} async-done(((bf16[2048,512]{1,0:T(8,128)(2,1)}), bf16[256,512]{1,0:T(8,128)(2,1)}) %reduce-scatter.20.cloned.1.call-update) | async-done | bytes 262160 | tf_op jit(solution)/shard_map/reduce_scatter | solution.py:292
  1586.9 44.3 %reduce-scatter.18.cloned.1.call-done = bf16[256,2048]{1,0:T(8,128)(2,1)} async-done(((bf16[1024,2048]{1,0:T(8,128)(2,1)}), bf16[256,2048]{1,0:T(8,128)(2,1)}) %reduce-scatter.18.cloned.1.call-update) | async-done | bytes 1048592 | tf_op jit(solution)/shard_map/reduce_scatter | solution.py:272
  1633.3 21.7 %all-reduce.3 = (bf16[2048]{0:T(1024)(128)(2,1)S(1)}, bf16[2048]{0:T(1024)(128)(2,1)S(1)}) all-reduce(bf16[2048]{0:T(1024)(128)(2,1)S(1)} %get-tuple-element.13, bf16[2048]{0:T(1024)(128)(2,1)S(1)} %copy-done.53), channel_id=6, replica_groups=mesh['dp'=8,'tensor'=4] {'dp'}, use_global_device_ids=true, to_apply=%region_15.16.clone | all-reduce | flops 4096 | bytes 16384
  1662.2 16.2 reduce-scatter.14.cloned.1.call-done
  (270 shorter events, 222.4 us)
Async XLA Ops:
  7.2 96.2 %all-gather.12.cloned.1.call-start = ((), (), s32[]{:S(2)}) async-start(), calls=%async_computation.11 | async-start | bytes 5242880 | tf_op jit(solution)/shard_map/all_gather | solution.py:136
  35.0 84.7 %all-gather.14.cloned.1.call-start = ((), (), s32[]{:S(2)}) async-start(), calls=%async_computation.12 | async-start | bytes 2359296 | tf_op jit(solution)/shard_map/all_gather | solution.py:160
  35.8 137.6 %all-gather.16.cloned.1.call-start = ((), (), s32[]{:S(2)}) async-start(), calls=%async_computation.13 | async-start | bytes 2359296 | tf_op jit(solution)/shard_map/all_gather | solution.py:163
  36.6 214.8 %reduce-scatter.12.cloned.1.call-start = ((), (), s32[]{:S(2)}) async-start(), calls=%async_computation.14 | async-start | bytes 10485760 | tf_op jit(solution)/shard_map/reduce_scatter | solution.py:193
  181.2 197.3 %all-gather.22.cloned.1.call-start = ((), (), s32[]{:S(2)}) async-start(), calls=%async_computation.17 | async-start | bytes 9437184 | tf_op jit(solution)/shard_map/all_gather | solution.py:168
  183.9 229.3 %all-gather.18.cloned.1.call-start = ((), (), s32[]{:S(2)}) async-start(), calls=%async_computation.15 | async-start | bytes 5242880 | tf_op jit(solution)/shard_map/all_gather | solution.py:136
  202.3 621.2 %copy-start.36 = (f32[8,1,256]{2,1,0:T(1,128)}, f32[8,1,256]{2,1,0:T(1,128)S(1)}, u32[]{:S(2)}) copy-start(f32[8,1,256]{2,1,0:T(1,128)S(1)} %convert_element_type.254) | copy-start | bytes 24580
  253.4 570.1 %copy-start.2 = (f32[256,2048]{1,0:T(8,128)}, f32[256,2048]{1,0:T(8,128)S(1)}, u32[]{:S(2)}) copy-start(f32[256,2048]{1,0:T(8,128)S(1)} %get-tuple-element.20) | copy-start | bytes 6291460
  253.4 570.1 %copy-start.51 = (f32[256]{0:T(256)}, f32[256]{0:T(256)S(1)}, u32[]{:S(2)}) copy-start(f32[256]{0:T(256)S(1)} %add_rsqrt_fusion) | copy-start | bytes 3076
  254.9 285.5 %all-gather.20.cloned.1.call-start = ((), (), s32[]{:S(2)}) async-start(), calls=%async_computation.16 | async-start | bytes 9437184 | tf_op jit(solution)/shard_map/all_gather | solution.py:167
  257.6 316.9 %all-gather.26.cloned.1.call-start = ((), (), s32[]{:S(2)}) async-start(), calls=%async_computation.20 | async-start | bytes 5242880 | tf_op jit(solution)/shard_map/all_gather | solution.py:140
  258.4 443.8 %all-gather.24.cloned.1.call-start = ((), (), s32[]{:S(2)}) async-start(), calls=%async_computation.18 | async-start | bytes 9437184 | tf_op jit(solution)/shard_map/all_gather | solution.py:169
  261.1 559.4 %reduce-scatter.16.cloned.1.call-start = ((), (), s32[]{:S(2)}) async-start(), calls=%async_computation.21 | async-start | bytes 10485760 | tf_op jit(solution)/shard_map/reduce_scatter | solution.py:228
  750.8 73.2 %copy-start.11 = (bf16[256,2048]{1,0:T(8,128)(2,1)S(1)}, bf16[256,2048]{1,0:T(8,128)(2,1)}, u32[]{:S(2)}) copy-start(bf16[256,2048]{1,0:T(8,128)(2,1)} %param.16) | copy-start | bytes 3145732
  750.8 118.5 %all-gather.28.cloned.1.call-start = ((), (), s32[]{:S(2)}) async-start(), calls=%async_computation.22 | async-start | bytes 5242880 | tf_op jit(solution)/shard_map/all_gather | solution.py:140
  825.7 185.7 %reduce-scatter.30.cloned.1.call-start = ((), (), s32[]{:S(2)}) async-start(), calls=%async_computation.29 | async-start | bytes 9437184 | tf_op jit(solution)/shard_map/reduce_scatter | solution.py:243
  840.0 321.5 %reduce-scatter.28.cloned.1.call-start = ((), (), s32[]{:S(2)}) async-start(), calls=%async_computation.28 | async-start | bytes 9437184 | tf_op jit(solution)/shard_map/reduce_scatter | solution.py:240
  854.2 457.8 %reduce-scatter.32.cloned.1.call-start = ((), (), s32[]{:S(2)}) async-start(), calls=%async_computation.30 | async-start | bytes 9437184 | tf_op jit(solution)/shard_map/reduce_scatter | solution.py:246
  868.6 509.0 %reduce-scatter.24.cloned.1.call-start = ((), (), s32[]{:S(2)}) async-start(), calls=%async_computation.26 | async-start | bytes 589824 | tf_op jit(solution)/shard_map/reduce_scatter | solution.py:298
  935.9 507.1 %reduce-scatter.22.cloned.1.call-start = ((), (), s32[]{:S(2)}) async-start(), calls=%async_computation.25 | async-start | bytes 589824 | tf_op jit(solution)/shard_map/reduce_scatter | solution.py:295
  955.8 558.5 %reduce-scatter.26.cloned.1.call-start = ((), (), s32[]{:S(2)}) async-start(), calls=%async_computation.27 | async-start | bytes 2359296 | tf_op jit(solution)/shard_map/reduce_scatter | solution.py:301
  961.8 623.3 %reduce-scatter.20.cloned.1.call-start = ((), (), s32[]{:S(2)}) async-start(), calls=%async_computation.24 | async-start | bytes 2359296 | tf_op jit(solution)/shard_map/reduce_scatter | solution.py:292
  978.6 652.7 %reduce-scatter.18.cloned.1.call-start = ((), (), s32[]{:S(2)}) async-start(), calls=%async_computation.23 | async-start | bytes 5242880 | tf_op jit(solution)/shard_map/reduce_scatter | solution.py:272
  986.2 692.2 %reduce-scatter.14.cloned.1.call-start = ((), (), s32[]{:S(2)}) async-start(), calls=%async_computation.19 | async-start | bytes 5242880 | tf_op jit(solution)/shard_map/reduce_scatter | solution.py:203
  1014.2 617.1 %copy-start.5 = (bf16[256,2048]{1,0:T(8,128)(2,1)S(1)}, bf16[256,2048]{1,0:T(8,128)(2,1)}, u32[]{:S(2)}) copy-start(bf16[256,2048]{1,0:T(8,128)(2,1)} %param.13) | copy-start | bytes 3145732
  1014.2 617.1 %copy-start.45 = (f32[8,1,256]{2,1,0:T(1,128)S(1)}, f32[8,1,256]{2,1,0:T(1,128)}, u32[]{:S(2)}) copy-start(f32[8,1,256]{2,1,0:T(1,128)} %copy-done.44) | copy-start | bytes 24580
  1014.2 617.1 %copy-start.55 = (f32[256]{0:T(256)S(1)}, f32[256]{0:T(256)}, u32[]{:S(2)}) copy-start(f32[256]{0:T(256)} %copy-done.54) | copy-start | bytes 3076
  1164.4 468.9 %copy-start.53 = (bf16[2048]{0:T(1024)(128)(2,1)S(1)}, bf16[2048]{0:T(1024)(128)(2,1)}, u32[]{:S(2)}) copy-start(bf16[2048]{0:T(1024)(128)(2,1)} %get-tuple-element.11) | copy-start | bytes 12292
  1164.4 514.0 %copy-start.3 = (f32[256,2048]{1,0:T(8,128)S(1)}, f32[256,2048]{1,0:T(8,128)}, u32[]{:S(2)}) copy-start(f32[256,2048]{1,0:T(8,128)} %copy-done.2) | copy-start | bytes 6291460
  1164.4 514.0 %copy-start.37 = (f32[8,1,256]{2,1,0:T(1,128)S(1)}, f32[8,1,256]{2,1,0:T(1,128)}, u32[]{:S(2)}) copy-start(f32[8,1,256]{2,1,0:T(1,128)} %copy-done.36) | copy-start | bytes 24580
  1164.4 514.0 %copy-start.52 = (f32[256]{0:T(256)S(1)}, f32[256]{0:T(256)}, u32[]{:S(2)}) copy-start(f32[256]{0:T(256)} %copy-done.51) | copy-start | bytes 3076
  1164.4 514.0 %copy-start.57 = (f32[256]{0:T(256)S(1)}, f32[256]{0:T(256)}, u32[]{:S(2)}) copy-start(f32[256]{0:T(256)} %copy-done.56) | copy-start | bytes 3076
  (60 other events, 843.8 us)
Sparse Core Ops, SparseCore 0:
  35.1 31.7 all-gather.11
  69.6 50.0 all-gather.13
  122.3 48.8 all-gather.15
  181.3 70.0 reduce-scatter.11
  254.0 124.4 all-gather.21
  380.5 32.6 all-gather.17
  415.8 124.4 all-gather.19
  541.9 32.6 all-gather.25
  577.2 124.9 all-gather.23
  750.9 69.5 reduce-scatter.15
  825.8 34.4 all-gather.27
  863.8 147.5 reduce-scatter.29
  1015.0 146.5 reduce-scatter.27
  1165.1 146.9 reduce-scatter.31
  1315.8 61.7 reduce-scatter.23
  1381.4 61.5 reduce-scatter.21
  1446.4 67.8 reduce-scatter.25
  1517.7 67.3 reduce-scatter.19
  1587.6 43.5 reduce-scatter.17
  1633.6 44.7 reduce-scatter.13
where the time goes:
time: 1700 us; the launch traced here: 1690 us
  waiting for transfers between devices  1170 us (69%)
  matrix products  263 us (15%)
  blocking collectives  133 us (8%)
  other arithmetic  87.9 us (5%)
    reduce_scatter x1, waiting for transfers between devices, local(): lax.psum_scatter(grad_w_down.astype(jnp.bfloat16), 'dp', scatter_dimensio...  148 us
    reduce_scatter x1, waiting for transfers between devices, local(): lax.psum_scatter(grad_w_gate.astype(jnp.bfloat16), 'dp', scatter_dimensio...  147 us
    all_gather x1, waiting for transfers between devices, local(): lax.all_gather(w_down.astype(jnp.bfloat16), 'dp', axis=1, tiled=True)  128 us
    all_gather x1, waiting for transfers between devices, local(): lax.all_gather(w_up.astype(jnp.bfloat16), 'dp', axis=0, tiled=True)  117 us
    all_gather x1, waiting for transfers between devices, local(): lax.all_gather(w_gate.astype(jnp.bfloat16), 'dp', axis=0, tiled=True)  112 us
    reduce_scatter x1, waiting for transfers between devices, local(): lax.psum_scatter(grad_w_out.astype(jnp.bfloat16), 'dp', scatter_dimension...  69.8 us
    reduce_scatter x1, waiting for transfers between devices, local(): lax.psum_scatter(back_product((grad_gate, grad_up), (gate_weight, up_weig...  69.7 us
    reduce_scatter x1, waiting for transfers between devices, local(): lax.psum_scatter(grad_w_query.astype(jnp.bfloat16), 'dp', scatter_dimensi...  69 us
  transfers between devices with their start and end apart: 20, of which 17 were waited for; matrix products, arithmetic and copies ran while one was open for 17% of the time, Pallas kernels for 0%

commit v1 on v0

--- a/solution.py
+++ b/solution.py
@@ -1,3 +1,4 @@
+import functools
 from functools import reduce
 import math
 import jax
@@ -8,6 +9,36 @@
 HEADS = 32
 KV_HEADS = 8
 HEAD_DIM = 64
+
+
+def map_view(field_in, out_dim):
+    field_in = jnp.moveaxis(field_in, 0, out_dim)
+    new = field_in.shape
+    return field_in.reshape(*new[:out_dim], new[out_dim] * new[out_dim + 1], *new[out_dim + 2 :])
+
+
+def _keep_up_chunk(obj, device_axis):
+    count_all = lax.axis_size(device_axis)
+    arr_next = obj[None]
+    for kk in range(count_all.bit_length() - 1):
+        view_out = 1 << kk
+        v_now = range(count_all)
+        tmp = map(lambda num: (num, num ^ view_out), v_now)
+        kept_arr = list(tmp)
+        lower = lax.ppermute(arr_next, device_axis, kept_arr)
+        current_arr = jnp.stack([arr_next, lower])
+        local_next = lax.axis_index(device_axis)
+        tall = local_next >> kk & 1
+        arr_next = jnp.where(tall == 0, current_arr, current_arr[::-1]).reshape(-1, *obj.shape)
+    return arr_next
+
+
+def show_loads_all(z_in, q_in, along_dim):
+    raw_out = _keep_up_chunk(z_in, q_in)
+    return map_view(raw_out, along_dim)
+
+
+advance_the_views = functools.partial(show_loads_all, q_in="dp", along_dim=0)
 
 
 def rotary_angles(positions, head_size):
@@ -165,7 +196,7 @@
     mlp_gain, gate_weight, up_weight, down_weight = (
         lax.all_gather(mlp_norm.astype(jnp.bfloat16), "dp", axis=0, tiled=True),
         lax.all_gather(w_gate.astype(jnp.bfloat16), "dp", axis=0, tiled=True),
-        lax.all_gather(w_up.astype(jnp.bfloat16), "dp", axis=0, tiled=True),
+        advance_the_views(w_up.astype(jnp.bfloat16)),
         lax.all_gather(w_down.astype(jnp.bfloat16), "dp", axis=1, tiled=True),
     )
     group = HEADS // KV_HEADS

time: 1700 us -> 1840 us (1.082)
  waiting for transfers between devices: 1170 us -> 1280 us
  other arithmetic: 87.9 us -> 122 us
    ppermute x0 -> x3, waiting for transfers between devices: none -> 427 us  [_keep_up_chunk(): lower = lax.ppermute(arr_next, device_axis, kept_arr)]
    reduce_scatter x1, waiting for transfers between devices: 9.3 us -> 147 us  [local(): lax.psum_scatter(grad_w_up.astype(jnp.bfloat16), 'dp', scatter_dimension=...]
    reduce_scatter x1, waiting for transfers between devices: 147 us -> 15.9 us  [local(): lax.psum_scatter(grad_w_gate.astype(jnp.bfloat16), 'dp', scatter_dimensio...]
    all_gather x1, waiting for transfers between devices: 128 us -> 0.01 us  [local(): lax.all_gather(w_down.astype(jnp.bfloat16), 'dp', axis=1, tiled=True)]
    all_gather x1, waiting for transfers between devices: 112 us -> 0.01 us  [local(): lax.all_gather(w_gate.astype(jnp.bfloat16), 'dp', axis=0, tiled=True)]
    all_gather x1, waiting for transfers between devices: 117 us -> 77.1 us  [local(): lax.all_gather(w_up.astype(jnp.bfloat16), 'dp', axis=0, tiled=True)]
    all_gather x2, waiting for transfers between devices: 19.7 us -> 0.02 us  [gather_grads(): return lax.all_gather(rows, 'tensor', axis=0, tiled=True)]
  transfers between devices with their start and end apart: 20 -> 23, of which waited for: 17 -> 17; matrix products, arithmetic and copies ran while one was open for 17% -> 19% of each run, Pallas kernels for 0% -> 0%
where the time goes in v1:
time: 1840 us; the launch traced here: 1830 us
  waiting for transfers between devices  1280 us (70%)
  matrix products  260 us (14%)
  blocking collectives  136 us (7%)
  other arithmetic  122 us (7%)
    ppermute x3, waiting for transfers between devices, _keep_up_chunk(): lower = lax.ppermute(arr_next, device_axis, kept_arr)  427 us
    reduce_scatter x1, waiting for transfers between devices, local(): lax.psum_scatter(grad_w_down.astype(jnp.bfloat16), 'dp', scatter_dimensio...  148 us
    reduce_scatter x1, waiting for transfers between devices, local(): lax.psum_scatter(grad_w_up.astype(jnp.bfloat16), 'dp', scatter_dimension=...  147 us
    all_gather x1, waiting for transfers between devices, local(): lax.all_gather(w_up.astype(jnp.bfloat16), 'dp', axis=0, tiled=True)  77.1 us
    reduce_scatter x1, waiting for transfers between devices, local(): lax.psum_scatter(back_product((grad_gate, grad_up), (gate_weight, up_weig...  69.7 us
    reduce_scatter x1, waiting for transfers between devices, local(): lax.psum_scatter(grad_w_query.astype(jnp.bfloat16), 'dp', scatter_dimensi...  69.6 us
    reduce_scatter x1, waiting for transfers between devices, local(): lax.psum_scatter(grad_w_out.astype(jnp.bfloat16), 'dp', scatter_dimension...  69.6 us
    reduce_scatter x1, waiting for transfers between devices, local(): lax.psum_scatter(grad_w_key.astype(jnp.bfloat16), 'dp', scatter_dimension...  64 us
  transfers between devices with their start and end apart: 23, of which 17 were waited for; matrix products, arithmetic and copies ran while one was open for 19% of the time, Pallas kernels for 0%

profile of v1, /device:TPU:0, one launch (start us, length us, event | category | flops | bytes accessed | tf_op | source)
XLA Modules:
  0.0 1830.9 jit_solution(4559965967047282567)
XLA Ops:
  9.9 22.3 %all-gather = bf16[8,1,256]{2,1,0:T(2,128)(2,1)S(1)} all-gather(bf16[1,1,256]{2,1,0:T(2,128)(2,1)S(1)} %reshape.235), channel_id=1, replica_groups=mesh['dp'=8,'tensor'=4] {'dp'}, dimensions={0}, use_global_device_ids=true | all-gather | bytes 4608 | tf_op jit(solution)/shard_map/all_gather | solution.py:190
  37.2 33.3 %all_gather.50 = bf16[2048,128]{1,0:T(8,128)(2,1)S(1)} all-gather(bf16[256,128]{1,0:T(8,128)(2,1)S(1)} %convert_element_type.200), channel_id=1, replica_groups=mesh['dp'=8,'tensor'=4] {'dp'}, dimensions={0}, use_global_device_ids=true | all-gather | bytes 589824 | tf_op jit(solution)/shard_map/all_gather | solution.py:192
  70.6 31.3 %all_gather.49 = bf16[2048,128]{1,0:T(8,128)(2,1)S(1)} all-gather(bf16[256,128]{1,0:T(8,128)(2,1)S(1)} %convert_element_type.198), channel_id=1, replica_groups=mesh['dp'=8,'tensor'=4] {'dp'}, dimensions={0}, use_global_device_ids=true | all-gather | bytes 589824 | tf_op jit(solution)/shard_map/all_gather | solution.py:193
  174.7 20.6 %all-gather.1 = bf16[8,1,256]{2,1,0:T(2,128)(2,1)S(1)} all-gather(bf16[1,1,256]{2,1,0:T(2,128)(2,1)S(1)} %reshape.237), channel_id=1, replica_groups=mesh['dp'=8,'tensor'=4] {'dp'}, dimensions={0}, use_global_device_ids=true | all-gather | bytes 4608 | tf_op jit(solution)/shard_map/all_gather | solution.py:197
  195.3 45.5 %reduce-scatter.12.cloned.1.call-done = f32[256,2048]{1,0:T(8,128)} async-done(((f32[1024,2048]{1,0:T(8,128)}), f32[256,2048]{1,0:T(8,128)}) %reduce-scatter.12.cloned.1.call-update) | async-done | bytes 2097168 | tf_op jit(solution)/shard_map/reduce_scatter | solution.py:224
  249.5 21.5 %collective-permute-done = bf16[1,256,2048]{2,1,0:T(8,128)(2,1)} collective-permute-done((bf16[1,256,2048]{2,1,0:T(8,128)(2,1)S(1)}, bf16[1,256,2048]{2,1,0:T(8,128)(2,1)}, u32[]{:S(2)}, u32[]{:S(2)}) %collective-permute-start) | collective-permute-done | bytes 1048608 | tf_op jit(solution)/shard_map/ppermute | solution.py:28
  278.2 77.3 %collective-permute-done.1 = bf16[2,256,2048]{2,1,0:T(8,128)(2,1)} collective-permute-done((bf16[2,256,2048]{2,1,0:T(8,128)(2,1)}, bf16[2,256,2048]{2,1,0:T(8,128)(2,1)}, u32[]{:S(2)}, u32[]{:S(2)}) %collective-permute-start.1) | collective-permute-done | bytes 2097184 | tf_op jit(solution)/shard_map/ppermute | solution.py:28
  362.9 327.8 %collective-permute-done.2 = bf16[4,256,2048]{2,1,0:T(8,128)(2,1)} collective-permute-done((bf16[4,256,2048]{2,1,0:T(8,128)(2,1)}, bf16[4,256,2048]{2,1,0:T(8,128)(2,1)}, u32[]{:S(2)}, u32[]{:S(2)}) %collective-permute-start.2) | collective-permute-done | bytes 4194336 | tf_op jit(solution)/shard_map/ppermute | solution.py:28
  698.3 14.3 reverse_select_fusion
  712.6 14.8 fusion.67
  727.4 20.5 %all-gather.18.cloned.1.call-done = bf16[1024,2048]{1,0:T(8,128)(2,1)} async-done(((bf16[256,2048]{1,0:T(8,128)(2,1)}), bf16[1024,2048]{1,0:T(8,128)(2,1)}) %all-gather.18.cloned.1.call-update) | async-done | bytes 4194320 | tf_op jit(solution)/shard_map/all_gather | solution.py:167
  747.9 15.5 fusion.66
  763.4 19.3 %multiply_convert_fusion = (bf16[1024,2048]{1,0:T(8,128)(2,1)}, bf16[1024,2048]{1,0:T(8,128)(2,1)}, bf16[1024,2048]{1,0:T(8,128)(2,1)}) fusion(f32[1024,2048]{1,0:T(8,128)} %fusion.67, f32[1024,2048]{1,0:T(8,128)} %fusion.66, bf16[1024,2048]{1,0:T(8,128)(2,1)S(1)} %copy-done.58, bf16[2048,2048]{1,0:T(8,128)(2,1)} %bitcast.167), kind=kOutput, calls=%fused_computation.29 | convolution fusion | flops 8621391872 | bytes 41943040 | tf_op jit(solution)/shard_map/dot_general | solution.py:230
  782.7 14.7 fusion.68
  797.5 77.1 %all-gather.26.cloned.1.call-done = bf16[2048,2048]{1,0:T(8,128)(2,1)} async-done(((bf16[256,2048]{1,0:T(8,128)(2,1)}), bf16[2048,2048]{1,0:T(8,128)(2,1)}) %all-gather.26.cloned.1.call-update) | async-done | bytes 8388624 | tf_op jit(solution)/shard_map/all_gather | solution.py:244
  874.6 15.7 convolution_add_fusion
  890.3 69.7 %reduce-scatter.16.cloned.1.call-done = f32[256,2048]{1,0:T(8,128)} async-done(((f32[1024,2048]{1,0:T(8,128)}), f32[256,2048]{1,0:T(8,128)}) %reduce-scatter.16.cloned.1.call-update) | async-done | bytes 2097168 | tf_op jit(solution)/shard_map/reduce_scatter | solution.py:259
  965.2 14.3 convolution_convert_fusion.2
  979.6 14.1 convolution_convert_fusion.1
  993.8 14.6 convolution_convert_fusion
  1026.0 12.3 fusion.2
  1119.0 13.9 convolution_convert_fusion.3
  1134.8 15.9 reduce-scatter.28.cloned.1.call-done
  1153.5 147.5 %reduce-scatter.30.cloned.1.call-done = bf16[256,2048]{1,0:T(8,128)(2,1)} async-done(((bf16[2048,2048]{1,0:T(8,128)(2,1)}), bf16[256,2048]{1,0:T(8,128)(2,1)}) %reduce-scatter.30.cloned.1.call-update) | async-done | bytes 1048592 | tf_op jit(solution)/shard_map/reduce_scatter | solution.py:274
  1303.7 147.6 %reduce-scatter.32.cloned.1.call-done = bf16[2048,256]{1,0:T(8,128)(2,1)} async-done(((bf16[2048,2048]{1,0:T(8,128)(2,1)}), bf16[2048,256]{1,0:T(8,128)(2,1)}) %reduce-scatter.32.cloned.1.call-update) | async-done | bytes 1048592 | tf_op jit(solution)/shard_map/reduce_scatter | solution.py:277
  1454.1 62.9 %reduce-scatter.24.cloned.1.call-done = bf16[256,128]{1,0:T(8,128)(2,1)} async-done(((bf16[2048,128]{1,0:T(8,128)(2,1)}), bf16[256,128]{1,0:T(8,128)(2,1)}) %reduce-scatter.24.cloned.1.call-update) | async-done | bytes 65552 | tf_op jit(solution)/shard_map/reduce_scatter | solution.py:329
  1518.5 64.0 %reduce-scatter.22.cloned.1.call-done = bf16[256,128]{1,0:T(8,128)(2,1)} async-done(((bf16[2048,128]{1,0:T(8,128)(2,1)}), bf16[256,128]{1,0:T(8,128)(2,1)}) %reduce-scatter.22.cloned.1.call-update) | async-done | bytes 65552 | tf_op jit(solution)/shard_map/reduce_scatter | solution.py:326
  1584.0 69.6 %reduce-scatter.20.cloned.1.call-done = bf16[256,512]{1,0:T(8,128)(2,1)} async-done(((bf16[2048,512]{1,0:T(8,128)(2,1)}), bf16[256,512]{1,0:T(8,128)(2,1)}) %reduce-scatter.20.cloned.1.call-update) | async-done | bytes 262160 | tf_op jit(solution)/shard_map/reduce_scatter | solution.py:323
  1655.4 69.6 %reduce-scatter.26.cloned.1.call-done = bf16[512,256]{1,0:T(8,128)(2,1)} async-done(((bf16[512,2048]{1,0:T(8,128)(2,1)}), bf16[512,256]{1,0:T(8,128)(2,1)}) %reduce-scatter.26.cloned.1.call-update) | async-done | bytes 262160 | tf_op jit(solution)/shard_map/reduce_scatter | solution.py:332
  1726.7 44.4 %reduce-scatter.18.cloned.1.call-done = bf16[256,2048]{1,0:T(8,128)(2,1)} async-done(((bf16[1024,2048]{1,0:T(8,128)(2,1)}), bf16[256,2048]{1,0:T(8,128)(2,1)}) %reduce-scatter.18.cloned.1.call-update) | async-done | bytes 1048592 | tf_op jit(solution)/shard_map/reduce_scatter | solution.py:303
  1773.2 21.7 %all-reduce.3 = (bf16[2048]{0:T(1024)(128)(2,1)S(1)}, bf16[2048]{0:T(1024)(128)(2,1)S(1)}) all-reduce(bf16[2048]{0:T(1024)(128)(2,1)S(1)} %get-tuple-element.13, bf16[2048]{0:T(1024)(128)(2,1)S(1)} %copy-done.52), channel_id=6, replica_groups=mesh['dp'=8,'tensor'=4] {'dp'}, use_global_device_ids=true, to_apply=%region_15.16.clone | all-reduce | flops 4096 | bytes 16384
  1802.1 16.2 reduce-scatter.14.cloned.1.call-done
  (273 shorter events, 244.8 us)
Async XLA Ops:
  7.2 97.4 %all-gather.14.cloned.1.call-start = ((), (), s32[]{:S(2)}) async-start(), calls=%async_computation.12 | async-start | bytes 2359296 | tf_op jit(solution)/shard_map/all_gather | solution.py:191
  9.1 96.2 %all-gather.12.cloned.1.call-start = ((), (), s32[]{:S(2)}) async-start(), calls=%async_computation.11 | async-start | bytes 5242880 | tf_op jit(solution)/shard_map/all_gather | solution.py:167
  36.3 125.2 %all-gather.16.cloned.1.call-start = ((), (), s32[]{:S(2)}) async-start(), calls=%async_computation.13 | async-start | bytes 2359296 | tf_op jit(solution)/shard_map/all_gather | solution.py:194
  37.1 203.8 %reduce-scatter.12.cloned.1.call-start = ((), (), s32[]{:S(2)}) async-start(), calls=%async_computation.14 | async-start | bytes 10485760 | tf_op jit(solution)/shard_map/reduce_scatter | solution.py:224
  169.2 543.4 %all-gather.24.cloned.1.call-start = ((), (), s32[]{:S(2)}) async-start(), calls=%async_computation.19 | async-start | bytes 5242880 | tf_op jit(solution)/shard_map/all_gather | solution.py:171
  169.8 542.8 %all-gather.22.cloned.1.call-start = ((), (), s32[]{:S(2)}) async-start(), calls=%async_computation.17 | async-start | bytes 9437184 | tf_op jit(solution)/shard_map/all_gather | solution.py:200
  171.8 555.6 %all-gather.20.cloned.1.call-start = ((), (), s32[]{:S(2)}) async-start(), calls=%async_computation.16 | async-start | bytes 9437184 | tf_op jit(solution)/shard_map/all_gather | solution.py:198
  174.6 573.3 %all-gather.18.cloned.1.call-start = ((), (), s32[]{:S(2)}) async-start(), calls=%async_computation.15 | async-start | bytes 5242880 | tf_op jit(solution)/shard_map/all_gather | solution.py:167
  195.3 767.6 %copy-start.35 = (f32[8,1,256]{2,1,0:T(1,128)}, f32[8,1,256]{2,1,0:T(1,128)S(1)}, u32[]{:S(2)}) copy-start(f32[8,1,256]{2,1,0:T(1,128)S(1)} %convert_element_type.254) | copy-start | bytes 24580
  242.8 720.1 %copy-start.1 = (f32[256,2048]{1,0:T(8,128)}, f32[256,2048]{1,0:T(8,128)S(1)}, u32[]{:S(2)}) copy-start(f32[256,2048]{1,0:T(8,128)S(1)} %get-tuple-element.20) | copy-start | bytes 6291460
  242.8 720.1 %copy-start.50 = (f32[256]{0:T(256)}, f32[256]{0:T(256)S(1)}, u32[]{:S(2)}) copy-start(f32[256]{0:T(256)S(1)} %add_rsqrt_fusion) | copy-start | bytes 3076
  244.3 630.3 %all-gather.26.cloned.1.call-start = ((), (), s32[]{:S(2)}) async-start(), calls=%async_computation.20 | async-start | bytes 9437184 | tf_op jit(solution)/shard_map/all_gather | solution.py:244
  246.1 24.9 %collective-permute-start = (bf16[1,256,2048]{2,1,0:T(8,128)(2,1)S(1)}, bf16[1,256,2048]{2,1,0:T(8,128)(2,1)}, u32[]{:S(2)}, u32[]{:S(2)}) collective-permute-start(bf16[1,256,2048]{2,1,0:T(8,128)(2,1)S(1)} %convert_bitcast_fusion.1), channel_id=1, source_target_pairs={{0,4},{4,0},{8,12},{12,8},{16,20},{20,16},{24,28},{28,24},{1,5},{5... | collective-permute-start | bytes 3145736 | tf_op jit(solution)/shard_map/ppermute | solution.py:28
  275.1 80.4 %collective-permute-start.1 = (bf16[2,256,2048]{2,1,0:T(8,128)(2,1)}, bf16[2,256,2048]{2,1,0:T(8,128)(2,1)}, u32[]{:S(2)}, u32[]{:S(2)}) collective-permute-start(bf16[2,256,2048]{2,1,0:T(8,128)(2,1)} %get-tuple-element.31), channel_id=1, source_target_pairs={{0,8},{4,12},{8,0},{12,4},{16,24},{20,28},{24,16},{28,20},{1,9},{5... | collective-permute-start | bytes 6291464 | tf_op jit(solution)/shard_map/ppermute | solution.py:28
  277.8 682.3 %reduce-scatter.16.cloned.1.call-start = ((), (), s32[]{:S(2)}) async-start(), calls=%async_computation.21 | async-start | bytes 10485760 | tf_op jit(solution)/shard_map/reduce_scatter | solution.py:259
  361.3 329.5 %collective-permute-start.2 = (bf16[4,256,2048]{2,1,0:T(8,128)(2,1)}, bf16[4,256,2048]{2,1,0:T(8,128)(2,1)}, u32[]{:S(2)}, u32[]{:S(2)}) collective-permute-start(bf16[4,256,2048]{2,1,0:T(8,128)(2,1)} %bitcast.26), channel_id=1, source_target_pairs={{0,16},{4,20},{8,24},{12,28},{16,0},{20,4},{24,8},{28,12},{1,17},{... | collective-permute-start | bytes 12582920 | tf_op jit(solution)/shard_map/ppermute | solution.py:28
  890.3 118.8 %all-gather.28.cloned.1.call-start = ((), (), s32[]{:S(2)}) async-start(), calls=%async_computation.22 | async-start | bytes 5242880 | tf_op jit(solution)/shard_map/all_gather | solution.py:171
  965.1 185.6 %reduce-scatter.28.cloned.1.call-start = ((), (), s32[]{:S(2)}) async-start(), calls=%async_computation.28 | async-start | bytes 9437184 | tf_op jit(solution)/shard_map/reduce_scatter | solution.py:271
  979.5 321.4 %reduce-scatter.30.cloned.1.call-start = ((), (), s32[]{:S(2)}) async-start(), calls=%async_computation.29 | async-start | bytes 9437184 | tf_op jit(solution)/shard_map/reduce_scatter | solution.py:274
  993.7 457.7 %reduce-scatter.32.cloned.1.call-start = ((), (), s32[]{:S(2)}) async-start(), calls=%async_computation.30 | async-start | bytes 9437184 | tf_op jit(solution)/shard_map/reduce_scatter | solution.py:277
  1008.4 508.6 %reduce-scatter.24.cloned.1.call-start = ((), (), s32[]{:S(2)}) async-start(), calls=%async_computation.26 | async-start | bytes 589824 | tf_op jit(solution)/shard_map/reduce_scatter | solution.py:329
  1084.0 498.5 %reduce-scatter.22.cloned.1.call-start = ((), (), s32[]{:S(2)}) async-start(), calls=%async_computation.25 | async-start | bytes 589824 | tf_op jit(solution)/shard_map/reduce_scatter | solution.py:326
  1098.6 555.0 %reduce-scatter.20.cloned.1.call-start = ((), (), s32[]{:S(2)}) async-start(), calls=%async_computation.24 | async-start | bytes 2359296 | tf_op jit(solution)/shard_map/reduce_scatter | solution.py:323
  1105.0 619.9 %reduce-scatter.26.cloned.1.call-start = ((), (), s32[]{:S(2)}) async-start(), calls=%async_computation.27 | async-start | bytes 2359296 | tf_op jit(solution)/shard_map/reduce_scatter | solution.py:332
  1111.0 660.1 %reduce-scatter.18.cloned.1.call-start = ((), (), s32[]{:S(2)}) async-start(), calls=%async_computation.23 | async-start | bytes 5242880 | tf_op jit(solution)/shard_map/reduce_scatter | solution.py:303
  1118.9 699.3 %reduce-scatter.14.cloned.1.call-start = ((), (), s32[]{:S(2)}) async-start(), calls=%async_computation.18 | async-start | bytes 5242880 | tf_op jit(solution)/shard_map/reduce_scatter | solution.py:234
  1153.5 617.7 %copy-start.4 = (bf16[256,2048]{1,0:T(8,128)(2,1)S(1)}, bf16[256,2048]{1,0:T(8,128)(2,1)}, u32[]{:S(2)}) copy-start(bf16[256,2048]{1,0:T(8,128)(2,1)} %param.13) | copy-start | bytes 3145732
  1153.5 617.7 %copy-start.44 = (f32[8,1,256]{2,1,0:T(1,128)S(1)}, f32[8,1,256]{2,1,0:T(1,128)}, u32[]{:S(2)}) copy-start(f32[8,1,256]{2,1,0:T(1,128)} %copy-done.43) | copy-start | bytes 24580
  1153.5 617.7 %copy-start.54 = (f32[256]{0:T(256)S(1)}, f32[256]{0:T(256)}, u32[]{:S(2)}) copy-start(f32[256]{0:T(256)} %copy-done.53) | copy-start | bytes 3076
  1303.7 514.5 %copy-start.2 = (f32[256,2048]{1,0:T(8,128)S(1)}, f32[256,2048]{1,0:T(8,128)}, u32[]{:S(2)}) copy-start(f32[256,2048]{1,0:T(8,128)} %copy-done.1) | copy-start | bytes 6291460
  1303.7 514.5 %copy-start.36 = (f32[8,1,256]{2,1,0:T(1,128)S(1)}, f32[8,1,256]{2,1,0:T(1,128)}, u32[]{:S(2)}) copy-start(f32[8,1,256]{2,1,0:T(1,128)} %copy-done.35) | copy-start | bytes 24580
  1303.7 514.5 %copy-start.51 = (f32[256]{0:T(256)S(1)}, f32[256]{0:T(256)}, u32[]{:S(2)}) copy-start(f32[256]{0:T(256)} %copy-done.50) | copy-start | bytes 3076
  (58 other events, 1785.4 us)
Sparse Core Ops, SparseCore 0:
  10.7 57.6 all-gather.13
  70.6 34.6 all-gather.11
  107.9 50.3 all-gather.15
  169.3 71.4 reduce-scatter.11
  242.2 34.4 all-gather.23
  279.2 274.9 all-gather.21
  556.3 156.0 all-gather.19
  714.6 33.2 all-gather.17
  750.1 124.4 all-gather.25
  890.4 69.5 reduce-scatter.15
  965.2 34.4 all-gather.27
  1003.2 147.4 reduce-scatter.27
  1154.3 146.5 reduce-scatter.29
  1304.4 146.8 reduce-scatter.31
  1455.1 61.7 reduce-scatter.23
  1520.7 61.7 reduce-scatter.21
  1585.9 67.6 reduce-scatter.19
  1657.0 67.9 reduce-scatter.25
  1727.5 43.6 reduce-scatter.17
  1773.5 44.7 reduce-scatter.13
